TPU v7x, 32 devices: a whole 2x2x4 slice. The times are simulated.
32 devices in a mesh: clip: 8 (over y, x, core), cap: 4 (over z).
Axes of the slice: x: 2, y: 2, z: 4, core: 2. Of those that a mesh axis runs over, the one named last changes fastest.
Arguments:
- teacher_audio: bfloat16 [6144, 512], P(('clip', 'cap')), may hold values from -2 to 2
- teacher_text: bfloat16 [6144, 512], P(('cap', 'clip')), may hold values from -2 to 2
- student_audio: bfloat16 [6144, 512], P(('clip', 'cap')), may hold values from -2 to 2
- student_text: bfloat16 [6144, 512], P(('cap', 'clip')), may hold values from -2 to 2
Outputs:
- audio_grad: float32 [6144, 512], P(('clip', 'cap'))
- text_grad: float32 [6144, 512], P(('cap', 'clip'))
All inputs are finite; a program needn't handle non-finite values.
Results may differ from a plain program's by a relative error of at most 0.0026.
Values may be sent and summed in bfloat16 or wider, within the bound.
A program may use at most 128 MiB of HBM per device.

v0:
```python
import jax
import jax.numpy as jnp
from jax import lax
from jax.sharding import PartitionSpec as P

ITERS = 3


def contract_rows(left_mat, right_mat):
    return lax.dot_general(
        left_mat, right_mat, (((1,), (1,)), ((), ())), preferred_element_type=jnp.float32
    )


def contract_first(left_mat, right_mat):
    return lax.dot_general(
        left_mat, right_mat, (((0,), (0,)), ((), ())), preferred_element_type=jnp.float32
    )


def body(teacher_audio, teacher_text, student_audio, student_text):
    audio_teacher, audio_student = (
        lax.all_gather(teacher_audio, "cap", axis=0, tiled=True),
        lax.all_gather(student_audio, "cap", axis=0, tiled=True),
    )
    text_teacher, text_student = (
        lax.all_gather(teacher_text, "clip", axis=0, tiled=True),
        lax.all_gather(student_text, "clip", axis=0, tiled=True),
    )
    teacher_logits = 10.0 * contract_rows(audio_teacher, text_teacher)
    student_logits = 10.0 * contract_rows(audio_student, text_student)
    teacher_max, student_max = lax.pmax(
        (jnp.max(teacher_logits, axis=1), jnp.max(student_logits, axis=1)), "cap"
    )
    student_exp = jnp.exp(student_logits - student_max[:, None])
    student_total = lax.psum(jnp.sum(student_exp, axis=1), "cap")
    kernel = jnp.exp(teacher_logits - teacher_max[:, None])
    weights_row = jnp.ones((kernel.shape[0],), jnp.float32)
    column_scale = jnp.ones((kernel.shape[1],), jnp.float32)
    for sweep_index in range(ITERS):
        column = lax.psum(jnp.dot(weights_row, kernel, precision=lax.Precision.HIGHEST), "clip")
        column_scale = 1.0 / column
        row_total = lax.psum(jnp.dot(kernel, column_scale, precision=lax.Precision.HIGHEST), "cap")
        weights_row = 1.0 / row_total
    target = weights_row[:, None] * kernel * column_scale[None, :]
    student_prob = student_exp / student_total[:, None]
    residual = (student_prob - target).astype(jnp.bfloat16)
    audio_grad = lax.psum_scatter(
        10.0 * jnp.dot(residual, text_student, preferred_element_type=jnp.float32),
        "cap",
        scatter_dimension=0,
        tiled=True,
    )
    text_grad = lax.psum_scatter(
        10.0 * contract_first(residual, audio_student), "clip", scatter_dimension=0, tiled=True
    )
    return (audio_grad, text_grad)


def solution(mesh):
    placed = (
        P(("clip", "cap"), None),
        P(("cap", "clip"), None),
        P(("clip", "cap"), None),
        P(("cap", "clip"), None),
    )
    return jax.shard_map(
        body,
        mesh=mesh,
        in_specs=placed,
        out_specs=(P(("clip", "cap"), None), P(("cap", "clip"), None)),
        check_vma=False,
    )
```

profile of v0, /device:TPU:0, one launch (start us, length us, event | category | flops | bytes accessed | tf_op | source)
XLA Modules:
  0.0 283.5 jit_solution(820184726141326755)
XLA Ops:
  7.2 0.0 all-gather.5.cloned.1.call-start
  7.2 0.7 all-gather.5.cloned.1.call-update
  7.9 0.0 all-gather.3.cloned.1.call-start
  7.9 0.7 all-gather.3.cloned.1.call-update
  8.6 0.0 reduce-scatter.3.cloned.1.call-start
  8.7 21.5 %all_gather.12 = bf16[768,512]{1,0:T(8,128)(2,1)S(1)} all-gather(bf16[192,512]{1,0:T(8,128)(2,1)} %param.6), channel_id=1, replica_groups=mesh['clip'=8,'cap'=4] {'cap'}, dimensions={0}, use_global_device_ids=true | all-gather | bytes 983040 | tf_op jit(solution)/shard_map/all_gather | solution.py:24
  30.2 17.9 %all_gather.14 = bf16[768,512]{1,0:T(8,128)(2,1)S(1)} all-gather(bf16[192,512]{1,0:T(8,128)(2,1)} %param.4), channel_id=1, replica_groups=mesh['clip'=8,'cap'=4] {'cap'}, dimensions={0}, use_global_device_ids=true | all-gather | bytes 983040 | tf_op jit(solution)/shard_map/all_gather | solution.py:23
  48.1 0.0 all-gather.5.cloned.1.call-done
  48.1 5.0 %multiply_reduce_fusion = (f32[768]{0:T(1024)S(1)}, f32[768,1536]{1,0:T(8,128)}) fusion(bf16[768,512]{1,0:T(8,128)(2,1)S(1)} %all_gather.14, bf16[1536,512]{1,0:T(8,128)(2,1)} %all-gather.5.cloned.1.call-done), kind=kOutput, calls=%fused_computation.3 | convolution fusion | flops 1210318080 | bytes 7080960 | tf_op jit(solution)/shard_map/dot_general | solution.py:10
  53.1 12.6 %all-gather.3.cloned.1.call-done = bf16[1536,512]{1,0:T(8,128)(2,1)} async-done(((bf16[192,512]{1,0:T(8,128)(2,1)}), bf16[1536,512]{1,0:T(8,128)(2,1)}) %all-gather.3.cloned.1.call-update) | async-done | bytes 1572880 | tf_op jit(solution)/shard_map/all_gather | solution.py:28
  65.7 5.0 %multiply_reduce_fusion.1 = (f32[768]{0:T(1024)S(1)}, f32[768,1536]{1,0:T(8,128)}) fusion(bf16[768,512]{1,0:T(8,128)(2,1)S(1)} %all_gather.12, bf16[1536,512]{1,0:T(8,128)(2,1)} %all-gather.3.cloned.1.call-done), kind=kOutput, calls=%fused_computation.4 | convolution fusion | flops 1210318080 | bytes 7080960 | tf_op jit(solution)/shard_map/dot_general | solution.py:10
  70.7 11.8 %all-reduce.1 = (f32[768]{0:T(1024)S(1)}, f32[768]{0:T(1024)S(1)}) all-reduce(f32[768]{0:T(1024)S(1)} %get-tuple-element.6, f32[768]{0:T(1024)S(1)} %get-tuple-element.8), channel_id=1, replica_groups=mesh['clip'=8,'cap'=4] {'cap'}, use_global_device_ids=true, to_apply=%region_5.0 | all-reduce | flops 1536 | bytes 12288 | tf_op jit(solution)/shard_map/pmax | solution.py:32
  82.5 5.3 %convolution_reduce_fusion.2 = f32[1536]{0:T(1024)S(1)} fusion(f32[768,1536]{1,0:T(8,128)} %get-tuple-element.7, f32[768]{0:T(1024)S(1)} %get-tuple-element.4), kind=kOutput, calls=%fused_computation.10 | convolution fusion | flops 16515072 | bytes 4727808 | tf_op jit(solution)/shard_map/dot_general | solution.py:41
  87.8 12.1 %psum.50 = f32[1536]{0:T(1024)S(1)} all-reduce(f32[1536]{0:T(1024)S(1)} %convolution_reduce_fusion.2), channel_id=1, replica_groups=mesh['clip'=8,'cap'=4] {'clip'}, use_global_device_ids=true, to_apply=%region_6.0 | all-reduce | flops 1536 | bytes 12288 | tf_op jit(solution)/shard_map/psum | solution.py:41
  99.9 6.9 %convolution_reduce_fusion.5 = f32[768]{0:T(1024)S(1)} fusion(f32[1536,1]{0,1:T(1,128)S(1)} %reshape.11, f32[768,1536]{1,0:T(8,128)} %get-tuple-element.7, f32[768]{0:T(1024)S(1)} %get-tuple-element.4), kind=kOutput, calls=%fused_computation.13 | convolution fusion | flops 16515072 | bytes 4730880 | tf_op jit(solution)/shard_map/dot_general | solution.py:43
  106.8 8.4 %psum.51 = f32[768]{0:T(1024)S(1)} all-reduce(f32[768]{0:T(1024)S(1)} %convolution_reduce_fusion.5), channel_id=1, replica_groups=mesh['clip'=8,'cap'=4] {'cap'}, use_global_device_ids=true, to_apply=%region_7.0 | all-reduce | flops 768 | bytes 6144 | tf_op jit(solution)/shard_map/psum | solution.py:43
  115.2 5.3 %convolution_reduce_fusion.1 = f32[1536]{0:T(1024)S(1)} fusion(f32[768,1]{0,1:T(1,128)S(1)} %reshape.13, f32[768,1536]{1,0:T(8,128)} %get-tuple-element.7, f32[768]{0:T(1024)S(1)} %get-tuple-element.4), kind=kOutput, calls=%fused_computation.9 | convolution fusion | flops 16515072 | bytes 4730880 | tf_op jit(solution)/shard_map/dot_general | solution.py:41
  120.5 12.0 %psum.52 = f32[1536]{0:T(1024)S(1)} all-reduce(f32[1536]{0:T(1024)S(1)} %convolution_reduce_fusion.1), channel_id=1, replica_groups=mesh['clip'=8,'cap'=4] {'clip'}, use_global_device_ids=true, to_apply=%region_8.0 | all-reduce | flops 1536 | bytes 12288 | tf_op jit(solution)/shard_map/psum | solution.py:41
  132.6 6.9 %convolution_reduce_fusion.4 = f32[768]{0:T(1024)S(1)} fusion(f32[1536,1]{0,1:T(1,128)S(1)} %reshape.15, f32[768,1536]{1,0:T(8,128)} %get-tuple-element.7, f32[768]{0:T(1024)S(1)} %get-tuple-element.4), kind=kOutput, calls=%fused_computation.12 | convolution fusion | flops 16515072 | bytes 4730880 | tf_op jit(solution)/shard_map/dot_general | solution.py:43
  139.5 10.4 %psum.53 = f32[768]{0:T(1024)S(1)} all-reduce(f32[768]{0:T(1024)S(1)} %convolution_reduce_fusion.4), channel_id=1, replica_groups=mesh['clip'=8,'cap'=4] {'cap'}, use_global_device_ids=true, to_apply=%region_9.0 | all-reduce | flops 768 | bytes 6144 | tf_op jit(solution)/shard_map/psum | solution.py:43
  149.9 5.3 %convolution_reduce_fusion = f32[1536]{0:T(1024)S(1)} fusion(f32[768,1]{0,1:T(1,128)S(1)} %reshape.17, f32[768,1536]{1,0:T(8,128)} %get-tuple-element.7, f32[768]{0:T(1024)S(1)} %get-tuple-element.4), kind=kOutput, calls=%fused_computation.8 | convolution fusion | flops 16515072 | bytes 4730880 | tf_op jit(solution)/shard_map/dot_general | solution.py:41
  155.2 12.3 %psum.54 = f32[1536]{0:T(1024)S(1)} all-reduce(f32[1536]{0:T(1024)S(1)} %convolution_reduce_fusion), channel_id=1, replica_groups=mesh['clip'=8,'cap'=4] {'clip'}, use_global_device_ids=true, to_apply=%region_10.0 | all-reduce | flops 1536 | bytes 12288 | tf_op jit(solution)/shard_map/psum | solution.py:41
  167.5 6.9 %convolution_reduce_fusion.3 = f32[768]{0:T(1024)S(1)} fusion(f32[1536,1]{0,1:T(1,128)S(1)} %reshape.19, f32[768,1536]{1,0:T(8,128)} %get-tuple-element.7, f32[768]{0:T(1024)S(1)} %get-tuple-element.4), kind=kOutput, calls=%fused_computation.11 | convolution fusion | flops 16515072 | bytes 4730880 | tf_op jit(solution)/shard_map/dot_general | solution.py:43
  174.4 3.2 %fusion = f32[768]{0:T(1024)S(1)} fusion(f32[768,1536]{1,0:T(8,128)} %get-tuple-element.9, f32[768]{0:T(1024)S(1)} %get-tuple-element.5), kind=kLoop, calls=%fused_computation.5 | loop fusion | flops 3538176 | bytes 4724736 | tf_op jit(solution)/shard_map/reduce_sum | solution.py:36
  177.7 8.5 %all-reduce = (f32[768]{0:T(1024)S(1)}, f32[768]{0:T(1024)S(1)}) all-reduce(f32[768]{0:T(1024)S(1)} %convolution_reduce_fusion.3, f32[768]{0:T(1024)S(1)} %fusion), channel_id=1, replica_groups=mesh['clip'=8,'cap'=4] {'cap'}, use_global_device_ids=true, to_apply=%region_11.0 | all-reduce | flops 1536 | bytes 12288 | tf_op jit(solution)/shard_map/psum | solution.py:43
  186.2 0.0 copy-start
  186.2 4.9 %subtract_convert_fusion = bf16[768,1536]{1,0:T(8,128)(2,1)S(1)} fusion(f32[768,1536]{1,0:T(8,128)} %get-tuple-element.9, f32[1536]{0:T(1024)S(1)} %broadcast_divide_fusion, f32[768]{0:T(1024)S(1)} %broadcast_divide_fusion.5, f32[768]{0:T(1024)S(1)} %get-tuple-element.3, f32[768]{0:T(1024)S(1)} %get-tuple-element.5, f32[768]{0:T(1024)S(1)} %get-tuple-element.4, ...), kind=kLoop, calls=%fused_computation | loop fusion | flops 10616832 | bytes 11814912 | tf_op jit(solution)/shard_map/convert_element_type | solution.py:47
  191.2 0.0 copy-done
  191.2 2.5 convolution_multiply_fusion.1
  193.7 0.0 reduce-scatter.3.cloned.1.call-update
  193.7 0.0 reduce-scatter.5.cloned.1.call-start
  193.8 3.1 %convolution_multiply_fusion = f32[1536,512]{1,0:T(8,128)} fusion(bf16[768,1536]{1,0:T(8,128)(2,1)S(1)} %subtract_convert_fusion, bf16[768,512]{1,0:T(8,128)(2,1)S(1)} %all_gather.12), kind=kOutput, calls=%fused_computation.6 | convolution fusion | flops 1208745984 | bytes 6291456 | tf_op jit(solution)/shard_map/dot_general | solution.py:16
  196.9 0.0 reduce-scatter.5.cloned.1.call-update
  196.9 31.3 %reduce-scatter.3.cloned.1.call-done = f32[192,512]{1,0:T(8,128)} async-done(((f32[768,512]{1,0:T(8,128)}), f32[192,512]{1,0:T(8,128)}) %reduce-scatter.3.cloned.1.call-update) | async-done | bytes 393232 | tf_op jit(solution)/shard_map/reduce_scatter | solution.py:48
  228.2 48.7 %reduce-scatter.5.cloned.1.call-done = f32[192,512]{1,0:T(8,128)} async-done(((f32[1536,512]{1,0:T(8,128)}), f32[192,512]{1,0:T(8,128)}) %reduce-scatter.5.cloned.1.call-update) | async-done | bytes 393232 | tf_op jit(solution)/shard_map/reduce_scatter | solution.py:54
  (11 shorter events, 0.1 us)
Async XLA Ops:
  7.2 41.0 %all-gather.5.cloned.1.call-start = ((), (), s32[]{:S(2)}) async-start(), calls=%async_computation.3 | async-start | bytes 1769472 | tf_op jit(solution)/shard_map/all_gather | solution.py:27
  7.9 57.8 %all-gather.3.cloned.1.call-start = ((), (), s32[]{:S(2)}) async-start(), calls=%async_computation.2 | async-start | bytes 1769472 | tf_op jit(solution)/shard_map/all_gather | solution.py:28
  8.6 219.5 %reduce-scatter.3.cloned.1.call-start = ((), (), s32[]{:S(2)}) async-start(), calls=%async_computation.4 | async-start | bytes 1966080 | tf_op jit(solution)/shard_map/reduce_scatter | solution.py:48
  186.2 5.0 %copy-start = (bf16[1536,512]{1,0:T(8,128)(2,1)S(1)}, bf16[1536,512]{1,0:T(8,128)(2,1)}, u32[]{:S(2)}) copy-start(bf16[1536,512]{1,0:T(8,128)(2,1)} %all-gather.3.cloned.1.call-done) | copy-start | bytes 4718596
  193.7 83.2 %reduce-scatter.5.cloned.1.call-start = ((), (), s32[]{:S(2)}) async-start(), calls=%async_computation.5 | async-start | bytes 3538944 | tf_op jit(solution)/shard_map/reduce_scatter | solution.py:54
Sparse Core Ops, SparseCore 0:
  9.8 28.2 all-gather.4
  40.1 25.5 all-gather.2
  193.9 34.2 reduce-scatter.2
  232.0 44.8 reduce-scatter.4
where the time goes:
time: 284 us; the launch traced here: 283 us
  blocking collectives  115 us (40%)
  waiting for transfers between devices  94 us (33%)
  matrix products  52.1 us (18%)
  between operations  13.9 us (5%)
  other arithmetic  8.21 us (3%)
    reduce_scatter x1, waiting for transfers between devices, body(): lax.psum_scatter(10.0 * contract_first(residual, audio_student), 'clip',...  48.7 us
    psum x3, blocking collectives, body(): lax.psum(jnp.dot(weights_row, kernel, precision=lax.Precision.HIGHEST), '...  36.4 us
    reduce_scatter x1, waiting for transfers between devices, body(): lax.psum_scatter(10.0 * jnp.dot(residual, text_student, preferred_element...  31.3 us
    psum x3, blocking collectives, body(): lax.psum(jnp.dot(kernel, column_scale, precision=lax.Precision.HIGHEST),...  27.3 us
    all_gather x1, blocking collectives, body(): lax.all_gather(student_audio, 'cap', axis=0, tiled=True)  21.5 us
    dot_general x3, matrix products, body(): jnp.dot(kernel, column_scale, precision=lax.Precision.HIGHEST)  20.8 us
    all_gather x1, blocking collectives, body(): lax.all_gather(teacher_audio, 'cap', axis=0, tiled=True)  17.9 us
    dot_general x3, matrix products, body(): jnp.dot(weights_row, kernel, precision=lax.Precision.HIGHEST)  15.8 us
  transfers between devices with their start and end apart: 4, of which 3 were waited for; matrix products, arithmetic and copies ran while one was open for 3% of the time, Pallas kernels for 0%

commit v1 on v0

--- a/solution.py
+++ b/solution.py
@@ -38,7 +38,9 @@
     weights_row = jnp.ones((kernel.shape[0],), jnp.float32)
     column_scale = jnp.ones((kernel.shape[1],), jnp.float32)
     for sweep_index in range(ITERS):
-        column = lax.psum(jnp.dot(weights_row, kernel, precision=lax.Precision.HIGHEST), "clip")
+        x = jnp.dot(weights_row, kernel, precision=lax.Precision.HIGHEST)
+        terms = lax.all_gather(x, "clip", axis=0, tiled=False)
+        column = terms.sum(axis=0)
         column_scale = 1.0 / column
         row_total = lax.psum(jnp.dot(kernel, column_scale, precision=lax.Precision.HIGHEST), "cap")
         weights_row = 1.0 / row_total

time: 284 us -> 274 us (0.965)
  blocking collectives: 115 us -> 105 us
    psum x3 -> x0, blocking collectives: 36.4 us -> none  [body(): lax.psum(jnp.dot(weights_row, kernel, precision=lax.Precision.HIGHEST), '...]
    all_gather x0 -> x3, blocking collectives: none -> 26.7 us  [body(): terms = lax.all_gather(x, 'clip', axis=0, tiled=False)]
where the time goes in v1:
time: 274 us
  blocking collectives  105 us (38%)
  waiting for transfers between devices  93.8 us (34%)
  matrix products  52.1 us (19%)
  between operations  13.9 us (5%)
  other arithmetic  8.34 us (3%)
    reduce_scatter x1, waiting for transfers between devices, body(): lax.psum_scatter(10.0 * contract_first(residual, audio_student), 'clip',...  48.7 us
    reduce_scatter x1, waiting for transfers between devices, body(): lax.psum_scatter(10.0 * jnp.dot(residual, text_student, preferred_element...  31.1 us
    psum x3, blocking collectives, body(): lax.psum(jnp.dot(kernel, column_scale, precision=lax.Precision.HIGHEST),...  27.3 us
    all_gather x3, blocking collectives, body(): terms = lax.all_gather(x, 'clip', axis=0, tiled=False)  26.7 us
    all_gather x1, blocking collectives, body(): lax.all_gather(student_audio, 'cap', axis=0, tiled=True)  21.5 us
    dot_general x3, matrix products, body(): jnp.dot(kernel, column_scale, precision=lax.Precision.HIGHEST)  20.8 us
    all_gather x1, blocking collectives, body(): lax.all_gather(teacher_audio, 'cap', axis=0, tiled=True)  17.9 us
    dot_general x3, matrix products, body(): x = jnp.dot(weights_row, kernel, precision=lax.Precision.HIGHEST)  15.8 us
  transfers between devices with their start and end apart: 4, of which 3 were waited for; matrix products, arithmetic and copies ran while one was open for 3% of the time, Pallas kernels for 0%

profile of v1, /device:TPU:0, one launch (start us, length us, event | category | flops | bytes accessed | tf_op | source)
XLA Modules:
  0.0 273.6 jit_solution(18262851329858294248)
XLA Ops:
  7.2 0.0 all-gather.11.cloned.1.call-start
  7.2 0.7 all-gather.11.cloned.1.call-update
  7.9 0.0 all-gather.9.cloned.1.call-start
  7.9 0.7 all-gather.9.cloned.1.call-update
  8.6 0.0 reduce-scatter.3.cloned.1.call-start
  8.7 21.5 %all_gather.30 = bf16[768,512]{1,0:T(8,128)(2,1)S(1)} all-gather(bf16[192,512]{1,0:T(8,128)(2,1)} %param.6), channel_id=1, replica_groups=mesh['clip'=8,'cap'=4] {'cap'}, dimensions={0}, use_global_device_ids=true | all-gather | bytes 983040 | tf_op jit(solution)/shard_map/all_gather | solution.py:24
  30.2 17.9 %all_gather.32 = bf16[768,512]{1,0:T(8,128)(2,1)S(1)} all-gather(bf16[192,512]{1,0:T(8,128)(2,1)} %param.4), channel_id=1, replica_groups=mesh['clip'=8,'cap'=4] {'cap'}, dimensions={0}, use_global_device_ids=true | all-gather | bytes 983040 | tf_op jit(solution)/shard_map/all_gather | solution.py:23
  48.1 0.0 all-gather.11.cloned.1.call-done
  48.1 5.0 %multiply_reduce_fusion = (f32[768]{0:T(1024)S(1)}, f32[768,1536]{1,0:T(8,128)}) fusion(bf16[768,512]{1,0:T(8,128)(2,1)S(1)} %all_gather.32, bf16[1536,512]{1,0:T(8,128)(2,1)} %all-gather.11.cloned.1.call-done), kind=kOutput, calls=%fused_computation.3 | convolution fusion | flops 1210318080 | bytes 7080960 | tf_op jit(solution)/shard_map/dot_general | solution.py:10
  53.1 12.6 %all-gather.9.cloned.1.call-done = bf16[1536,512]{1,0:T(8,128)(2,1)} async-done(((bf16[192,512]{1,0:T(8,128)(2,1)}), bf16[1536,512]{1,0:T(8,128)(2,1)}) %all-gather.9.cloned.1.call-update) | async-done | bytes 1572880 | tf_op jit(solution)/shard_map/all_gather | solution.py:28
  65.7 5.0 %multiply_reduce_fusion.1 = (f32[768]{0:T(1024)S(1)}, f32[768,1536]{1,0:T(8,128)}) fusion(bf16[768,512]{1,0:T(8,128)(2,1)S(1)} %all_gather.30, bf16[1536,512]{1,0:T(8,128)(2,1)} %all-gather.9.cloned.1.call-done), kind=kOutput, calls=%fused_computation.4 | convolution fusion | flops 1210318080 | bytes 7080960 | tf_op jit(solution)/shard_map/dot_general | solution.py:10
  70.7 11.8 %all-reduce.1 = (f32[768]{0:T(1024)S(1)}, f32[768]{0:T(1024)S(1)}) all-reduce(f32[768]{0:T(1024)S(1)} %get-tuple-element.6, f32[768]{0:T(1024)S(1)} %get-tuple-element.8), channel_id=1, replica_groups=mesh['clip'=8,'cap'=4] {'cap'}, use_global_device_ids=true, to_apply=%region_5.0 | all-reduce | flops 1536 | bytes 12288 | tf_op jit(solution)/shard_map/pmax | solution.py:32
  82.5 5.3 %convolution_bitcast_fusion.2 = f32[1,1,1536]{2,1,0:T(1,128)S(1)} fusion(f32[768,1536]{1,0:T(8,128)} %get-tuple-element.7, f32[768]{0:T(1024)S(1)} %get-tuple-element.4), kind=kOutput, calls=%fused_computation.9 | convolution fusion | flops 16515072 | bytes 4727808 | tf_op jit(solution)/shard_map/dot_general | solution.py:41
  87.7 9.1 %all-gather.3 = f32[8,1,1536]{2,1,0:T(1,128)S(1)} all-gather(f32[1,1,1536]{2,1,0:T(1,128)S(1)} %convolution_bitcast_fusion.2), channel_id=2, replica_groups=mesh['clip'=8,'cap'=4] {'clip'}, dimensions={0}, use_global_device_ids=true | all-gather | bytes 55296 | tf_op jit(solution)/shard_map/all_gather | solution.py:42
  96.9 6.9 %convolution_reduce_fusion.2 = f32[768]{0:T(1024)S(1)} fusion(f32[1536,1]{0,1:T(1,128)S(1)} %reshape.25, f32[768,1536]{1,0:T(8,128)} %get-tuple-element.7, f32[768]{0:T(1024)S(1)} %get-tuple-element.4), kind=kOutput, calls=%fused_computation.13 | convolution fusion | flops 16515072 | bytes 4730880 | tf_op jit(solution)/shard_map/dot_general | solution.py:45
  103.9 8.4 %psum.29 = f32[768]{0:T(1024)S(1)} all-reduce(f32[768]{0:T(1024)S(1)} %convolution_reduce_fusion.2), channel_id=1, replica_groups=mesh['clip'=8,'cap'=4] {'cap'}, use_global_device_ids=true, to_apply=%region_7.0 | all-reduce | flops 768 | bytes 6144 | tf_op jit(solution)/shard_map/psum | solution.py:45
  112.3 5.3 %convolution_bitcast_fusion.1 = f32[1,1,1536]{2,1,0:T(1,128)S(1)} fusion(f32[768,1]{0,1:T(1,128)S(1)} %reshape.27, f32[768,1536]{1,0:T(8,128)} %get-tuple-element.7, f32[768]{0:T(1024)S(1)} %get-tuple-element.4), kind=kOutput, calls=%fused_computation.8 | convolution fusion | flops 16515072 | bytes 4730880 | tf_op jit(solution)/shard_map/dot_general | solution.py:41
  117.5 8.2 %all-gather.4 = f32[8,1,1536]{2,1,0:T(1,128)S(1)} all-gather(f32[1,1,1536]{2,1,0:T(1,128)S(1)} %convolution_bitcast_fusion.1), channel_id=3, replica_groups=mesh['clip'=8,'cap'=4] {'clip'}, dimensions={0}, use_global_device_ids=true | all-gather | bytes 55296 | tf_op jit(solution)/shard_map/all_gather | solution.py:42
  125.8 6.9 %convolution_reduce_fusion.1 = f32[768]{0:T(1024)S(1)} fusion(f32[1536,1]{0,1:T(1,128)S(1)} %reshape.29, f32[768,1536]{1,0:T(8,128)} %get-tuple-element.7, f32[768]{0:T(1024)S(1)} %get-tuple-element.4), kind=kOutput, calls=%fused_computation.12 | convolution fusion | flops 16515072 | bytes 4730880 | tf_op jit(solution)/shard_map/dot_general | solution.py:45
  132.7 10.4 %psum.30 = f32[768]{0:T(1024)S(1)} all-reduce(f32[768]{0:T(1024)S(1)} %convolution_reduce_fusion.1), channel_id=1, replica_groups=mesh['clip'=8,'cap'=4] {'cap'}, use_global_device_ids=true, to_apply=%region_9.0 | all-reduce | flops 768 | bytes 6144 | tf_op jit(solution)/shard_map/psum | solution.py:45
  143.1 5.3 %convolution_bitcast_fusion = f32[1,1,1536]{2,1,0:T(1,128)S(1)} fusion(f32[768,1]{0,1:T(1,128)S(1)} %reshape.31, f32[768,1536]{1,0:T(8,128)} %get-tuple-element.7, f32[768]{0:T(1024)S(1)} %get-tuple-element.4), kind=kOutput, calls=%fused_computation.7 | convolution fusion | flops 16515072 | bytes 4730880 | tf_op jit(solution)/shard_map/dot_general | solution.py:41
  148.4 9.3 %all-gather.5 = f32[8,1,1536]{2,1,0:T(1,128)S(1)} all-gather(f32[1,1,1536]{2,1,0:T(1,128)S(1)} %convolution_bitcast_fusion), channel_id=4, replica_groups=mesh['clip'=8,'cap'=4] {'clip'}, dimensions={0}, use_global_device_ids=true | all-gather | bytes 55296 | tf_op jit(solution)/shard_map/all_gather | solution.py:42
  157.8 6.9 %convolution_reduce_fusion = f32[768]{0:T(1024)S(1)} fusion(f32[1536,1]{0,1:T(1,128)S(1)} %reshape.33, f32[768,1536]{1,0:T(8,128)} %get-tuple-element.7, f32[768]{0:T(1024)S(1)} %get-tuple-element.4), kind=kOutput, calls=%fused_computation.11 | convolution fusion | flops 16515072 | bytes 4730880 | tf_op jit(solution)/shard_map/dot_general | solution.py:45
  164.8 3.2 %fusion = f32[768]{0:T(1024)S(1)} fusion(f32[768,1536]{1,0:T(8,128)} %get-tuple-element.9, f32[768]{0:T(1024)S(1)} %get-tuple-element.5), kind=kLoop, calls=%fused_computation.5 | loop fusion | flops 3538176 | bytes 4724736 | tf_op jit(solution)/shard_map/reduce_sum | solution.py:36
  168.0 8.5 %all-reduce = (f32[768]{0:T(1024)S(1)}, f32[768]{0:T(1024)S(1)}) all-reduce(f32[768]{0:T(1024)S(1)} %convolution_reduce_fusion, f32[768]{0:T(1024)S(1)} %fusion), channel_id=1, replica_groups=mesh['clip'=8,'cap'=4] {'cap'}, use_global_device_ids=true, to_apply=%region_11.0 | all-reduce | flops 1536 | bytes 12288 | tf_op jit(solution)/shard_map/psum | solution.py:45
  176.5 0.0 copy-start
  176.6 4.9 %subtract_convert_fusion = bf16[768,1536]{1,0:T(8,128)(2,1)S(1)} fusion(f32[768,1536]{1,0:T(8,128)} %get-tuple-element.9, f32[1536]{0:T(1024)S(1)} %broadcast_divide_fusion, f32[768]{0:T(1024)S(1)} %broadcast_divide_fusion.5, f32[768]{0:T(1024)S(1)} %get-tuple-element.3, f32[768]{0:T(1024)S(1)} %get-tuple-element.5, f32[768]{0:T(1024)S(1)} %get-tuple-element.4, ...), kind=kLoop, calls=%fused_computation | loop fusion | flops 10616832 | bytes 11814912 | tf_op jit(solution)/shard_map/convert_element_type | solution.py:49
  181.5 0.0 copy-done
  181.5 2.5 convolution_multiply_fusion.1
  184.0 0.0 reduce-scatter.3.cloned.1.call-update
  184.1 0.0 reduce-scatter.5.cloned.1.call-start
  184.1 3.1 %convolution_multiply_fusion = f32[1536,512]{1,0:T(8,128)} fusion(bf16[768,1536]{1,0:T(8,128)(2,1)S(1)} %subtract_convert_fusion, bf16[768,512]{1,0:T(8,128)(2,1)S(1)} %all_gather.30), kind=kOutput, calls=%fused_computation.6 | convolution fusion | flops 1208745984 | bytes 6291456 | tf_op jit(solution)/shard_map/dot_general | solution.py:16
  187.2 0.0 reduce-scatter.5.cloned.1.call-update
  187.2 31.1 %reduce-scatter.3.cloned.1.call-done = f32[192,512]{1,0:T(8,128)} async-done(((f32[768,512]{1,0:T(8,128)}), f32[192,512]{1,0:T(8,128)}) %reduce-scatter.3.cloned.1.call-update) | async-done | bytes 393232 | tf_op jit(solution)/shard_map/reduce_scatter | solution.py:50
  218.3 48.7 %reduce-scatter.5.cloned.1.call-done = f32[192,512]{1,0:T(8,128)} async-done(((f32[1536,512]{1,0:T(8,128)}), f32[192,512]{1,0:T(8,128)}) %reduce-scatter.5.cloned.1.call-update) | async-done | bytes 393232 | tf_op jit(solution)/shard_map/reduce_scatter | solution.py:56
  (14 shorter events, 0.2 us)
Async XLA Ops:
  7.2 41.0 %all-gather.11.cloned.1.call-start = ((), (), s32[]{:S(2)}) async-start(), calls=%async_computation.3 | async-start | bytes 1769472 | tf_op jit(solution)/shard_map/all_gather | solution.py:27
  7.9 57.8 %all-gather.9.cloned.1.call-start = ((), (), s32[]{:S(2)}) async-start(), calls=%async_computation.2 | async-start | bytes 1769472 | tf_op jit(solution)/shard_map/all_gather | solution.py:28
  8.6 209.7 %reduce-scatter.3.cloned.1.call-start = ((), (), s32[]{:S(2)}) async-start(), calls=%async_computation.4 | async-start | bytes 1966080 | tf_op jit(solution)/shard_map/reduce_scatter | solution.py:50
  176.5 5.0 %copy-start = (bf16[1536,512]{1,0:T(8,128)(2,1)S(1)}, bf16[1536,512]{1,0:T(8,128)(2,1)}, u32[]{:S(2)}) copy-start(bf16[1536,512]{1,0:T(8,128)(2,1)} %all-gather.9.cloned.1.call-done) | copy-start | bytes 4718596
  184.1 83.0 %reduce-scatter.5.cloned.1.call-start = ((), (), s32[]{:S(2)}) async-start(), calls=%async_computation.5 | async-start | bytes 3538944 | tf_op jit(solution)/shard_map/reduce_scatter | solution.py:56
Sparse Core Ops, SparseCore 0:
  9.8 28.2 all-gather.10
  40.1 25.5 all-gather.8
  184.2 34.1 reduce-scatter.2
  222.1 44.8 reduce-scatter.4
